TPU v7x, 32 devices: a whole 2x2x4 slice. The times are simulated.
32 devices in a mesh: inputs: 8 (over z, y), tm: 4 (over x, core).
Axes of the slice: x: 2, y: 2, z: 4, core: 2. Of those that a mesh axis runs over, the one named last changes fastest.
Arguments:
- voltages: bfloat16 [128, 131072], P('inputs', 'tm'), may hold values from -8 to 8
- pfb_taps: float32 [8, 512], replicated, may hold values from -2 to 2
Outputs:
- visibilities: float32 [256, 1, 2, 128, 128], P(('inputs', 'tm'))
All inputs are finite; a program needn't handle non-finite values.
Results may differ from a plain program's by a relative error of at most 0.002.
Values may be sent and summed in bfloat16 or wider, within the bound.
No kernel may reach another device: no remote copies, remote signals or barrier semaphores. Data moves between devices by JAX's collectives and lax.ppermute only.
A program may use at most 128 MiB of HBM per device.

v0:
```python
import jax
import jax.numpy as jnp
from jax import lax
from jax.sharding import PartitionSpec as P

F = 256
TAPS = 8
TILE = 128
FRAME = 512


def from_behind(value, axis, steps):
    count = lax.axis_size(axis)
    initial, last = (max(0, -steps), min(count, count - steps))
    return lax.ppermute(value, axis, [(source, source + steps) for source in range(initial, last)])


def dft_table(chans, length):
    rows = jnp.arange(2 * chans, dtype=jnp.int32)
    freq = rows // 2
    part = rows % 2
    samp = jnp.arange(length, dtype=jnp.int32)
    phase = freq[:, None] * samp[None, :] % length
    angle = 2.0 * jnp.pi / length * phase.astype(jnp.float32)
    vals = jnp.where(part[:, None] == 0, jnp.cos(angle), -jnp.sin(angle))
    return (vals * (1.0 / length**0.5)).astype(jnp.bfloat16)


def tile_sums(spec, scale):
    left = jnp.concatenate([spec[:, 0], spec[:, 1]], axis=-1)
    twisted = jnp.concatenate([spec[:, 1], -spec[:, 0]], axis=-1)
    count_in = left.shape[1]
    blocks = count_in // TILE
    chans = left.shape[0]
    real_rows = []
    imag_rows = []
    for first in range(blocks):
        lower = first * TILE
        cols = left[:, lower:]
        real_part = jnp.einsum(
            "cik,cjk->cij", left[:, lower : lower + TILE], cols, preferred_element_type=jnp.float32
        )
        imag_part = jnp.einsum(
            "cik,cjk->cij",
            twisted[:, lower : lower + TILE],
            cols,
            preferred_element_type=jnp.float32,
        )
        count = blocks - first
        real_rows.append(real_part.reshape(chans, TILE, count, TILE).transpose(0, 2, 1, 3))
        imag_rows.append(imag_part.reshape(chans, TILE, count, TILE).transpose(0, 2, 1, 3))
    real_all = jnp.concatenate(real_rows, axis=1)
    imag_all = jnp.concatenate(imag_rows, axis=1)
    return jnp.stack([real_all, imag_all], axis=2) * scale


def on_device(voltages, pfb_taps):
    inp_local = voltages.shape[0]
    frames_local = voltages.shape[1] // FRAME
    previous = from_behind(voltages[:, voltages.shape[1] - (TAPS - 1) * FRAME :], "tm", 1)
    extended = jnp.concatenate([previous, voltages], axis=1).reshape(
        inp_local, frames_local + TAPS - 1, FRAME
    )
    filtered = jnp.zeros((inp_local, frames_local, FRAME), jnp.float32)
    for tap in range(TAPS):
        filtered = filtered + pfb_taps[tap][None, None, :] * extended[
            :, tap : tap + frames_local, :
        ].astype(jnp.float32)
    filtered = filtered.astype(jnp.bfloat16)
    table = dft_table(F, FRAME)
    spectra = jnp.einsum("kn,itn->kit", table, filtered, preferred_element_type=jnp.float32)
    spectra = spectra.astype(jnp.bfloat16).reshape(F, 2, inp_local, frames_local)
    blocks_time = lax.axis_size("tm")
    scale = 1.0 / (frames_local * blocks_time)
    turned = lax.all_to_all(
        lax.all_to_all(spectra, "inputs", split_axis=0, concat_axis=2, tiled=True),
        "tm",
        split_axis=0,
        concat_axis=3,
        tiled=True,
    )
    return tile_sums(turned, scale)


def solution(mesh):
    in_specs = (P("inputs", "tm"), P())
    out_specs = P(("inputs", "tm"), None, None, None, None)
    return jax.shard_map(
        on_device, mesh=mesh, in_specs=in_specs, out_specs=out_specs, check_vma=False
    )
```

profile of v0, /device:TPU:0, one launch (start us, length us, event | category | flops | bytes accessed | tf_op | source)
XLA Modules:
  0.0 76.3 jit_solution(17021184768935166234)
XLA Ops:
  0.0 0.9 %slice.60 = bf16[16,3584]{1,0:T(8,128)(2,1)S(1)} slice(bf16[16,32768]{1,0:T(8,128)(2,1)} %param.2), slice={[0:16], [29184:32768]} | slice | bytes 229376 | tf_op jit(solution)/shard_map/slice | solution.py:60
  0.9 2.4 %collective-permute-start = (bf16[16,3584]{1,0:T(8,128)(2,1)S(1)}, bf16[16,3584]{1,0:T(8,128)(2,1)S(1)}, u32[]{:S(2)}, u32[]{:S(2)}) collective-permute-start(bf16[16,3584]{1,0:T(8,128)(2,1)S(1)} %slice.60), channel_id=1, source_target_pairs={{0,1},{1,2},{2,3},{4,5},{5,6},{6,7},{8,9},{9,10},{10,11},{12,13},{... | collective-permute-start | bytes 344072 | tf_op jit(solution)/shard_map/ppermute | solution.py:15
  3.3 1.0 %fusion.32 = (f32[1,512]{1,0:T(1,128)S(1)}, f32[1,512]{1,0:T(1,128)S(1)}, f32[1,512]{1,0:T(1,128)S(1)}, f32[1,512]{1,0:T(1,128)S(1)}, f32[1,512]{1,0:T(1,128)S(1...) fusion(f32[8,512]{1,0:T(8,128)} %param.3), kind=kLoop, calls=%fused_computation.48 | loop fusion | bytes 32768 | tf_op jit(solution)/shard_map/slice | solution.py:66
  4.4 0.0 collective-permute-done
  4.4 1.3 %pad_maximum_fusion = bf16[16,36352]{1,0:T(8,128)(2,1)S(1)} fusion(bf16[16,32768]{1,0:T(8,128)(2,1)} %param.2, bf16[16,3584]{1,0:T(8,128)(2,1)S(1)} %collective-permute-done), kind=kLoop, calls=%fused_computation.7 | loop fusion | flops 2326528 | bytes 2326528 | tf_op jit(solution)/shard_map/concatenate | solution.py:61
  5.7 0.7 reshape.74
  6.4 6.5 %convolution_convert_fusion = bf16[512,16,64]{0,2,1:T(8,128)(2,1)S(1)} fusion(bf16[16,71,512]{2,1,0:T(8,128)(2,1)S(1)} %reshape.74, f32[512]{0:T(512)S(1)} %bitcast.42, f32[512]{0:T(512)S(1)} %bitcast.43, f32[512]{0:T(512)S(1)} %bitcast.37, f32[512]{0:T(512)S(1)} %bitcast.38, f32[512]{0:T(512)S(1)} %bitcast.39, f32[512]{0:T(512)S(1)} %bitcast.40, ...), kind=kOutput, calls=%fused_computation.4 | convolution fusion | flops 554696704 | bytes 9456128 | tf_op jit(solution)/shard_map/kn,itn->kit/dot_general | solution.py:71
  12.9 2.0 %copy.11 = bf16[512,16,64]{2,1,0:T(8,128)(2,1)S(1)} copy(bf16[512,16,64]{0,2,1:T(8,128)(2,1)S(1)} %convolution_convert_fusion) | data formatting | bytes 2097152 | tf_op jit(solution)/shard_map/convert_element_type | solution.py:72
  15.0 1.7 %reshape.77 = bf16[8,2,32768]{2,1,0:T(2,128)(2,1)S(1)} reshape(bf16[256,2,16,64]{3,2,1,0:T(8,128)(2,1)S(1)} %bitcast.27) | data formatting | bytes 2097152
  16.7 32.5 %all_to_all.36 = bf16[8,2,32768]{2,1,0:T(2,128)(2,1)} all-to-all(bf16[8,2,32768]{2,1,0:T(2,128)(2,1)S(1)} %reshape.77), channel_id=1, replica_groups=mesh['inputs'=8,'tm'=4] {'inputs'}, dimensions={0} | all-to-all | bytes 2097152 | tf_op jit(solution)/shard_map/all_to_all | solution.py:76
  49.1 3.1 %reshape.78 = bf16[256,2,16,64]{3,2,1,0:T(8,128)(2,1)S(1)} reshape(bf16[8,2,32768]{2,1,0:T(2,128)(2,1)} %all_to_all.36) | data formatting | bytes 2097152
  52.2 2.0 %copy.12 = bf16[8,32,2,16,64]{4,3,0,2,1:T(8,128)(2,1)} copy(bf16[8,32,2,16,64]{4,3,2,1,0:T(8,128)(2,1)S(1)} %bitcast.28) | data formatting | bytes 2097152 | tf_op jit(solution)/shard_map/all_to_all | solution.py:76
  54.2 2.0 %copy.13 = bf16[32,2,128,64]{2,3,1,0:T(8,128)(2,1)S(1)} copy(bf16[32,2,128,64]{3,2,1,0:T(8,128)(2,1)} %bitcast.29) | data formatting | bytes 2097152 | tf_op jit(solution)/shard_map/all_to_all | solution.py:76
  56.2 17.4 %all_to_all.37 = bf16[32,2,128,64]{2,3,1,0:T(8,128)(2,1)S(1)} all-to-all(bf16[32,2,128,64]{2,3,1,0:T(8,128)(2,1)S(1)} %copy.13), channel_id=1, replica_groups=mesh['inputs'=8,'tm'=4] {'tm'}, dimensions={0} | all-to-all | bytes 2097152 | tf_op jit(solution)/shard_map/all_to_all | solution.py:75
  73.6 0.1 copy.14
  73.7 0.1 fusion.31
  73.8 0.2 copy.19
  74.0 0.2 copy.18
  74.3 0.4 convolution_bitcast_fusion.1
  74.7 0.4 convolution_bitcast_fusion
  75.2 0.1 maximum_multiply_fusion
  75.3 1.1 %copy.17 = f32[8,1,2,128,128]{4,3,2,1,0:T(8,128)} copy(f32[8,1,2,128,128]{4,3,0,2,1:T(8,128)S(1)} %maximum_multiply_fusion) | data formatting | bytes 2097152 | tf_op jit(solution)/shard_map/mul | solution.py:54
  (3 shorter events, 0.0 us)
Async XLA Ops:
  0.9 3.5 %collective-permute-start = (bf16[16,3584]{1,0:T(8,128)(2,1)S(1)}, bf16[16,3584]{1,0:T(8,128)(2,1)S(1)}, u32[]{:S(2)}, u32[]{:S(2)}) collective-permute-start(bf16[16,3584]{1,0:T(8,128)(2,1)S(1)} %slice.60), channel_id=1, source_target_pairs={{0,1},{1,2},{2,3},{4,5},{5,6},{6,7},{8,9},{9,10},{10,11},{12,13},{... | collective-permute-start | bytes 344072 | tf_op jit(solution)/shard_map/ppermute | solution.py:15
where the time goes:
time: 76.7 us; the launch traced here: 76.3 us
  blocking collectives  49.9 us (65%)
  local copies, waits for them, and re-layouts  15.1 us (20%)
  matrix products  7.4 us (10%)
  starting transfers between devices  2.39 us (3%)
  other arithmetic  1.43 us (2%)
    all_to_all x1, blocking collectives, on_device(): lax.all_to_all(spectra, 'inputs', split_axis=0, concat_axis=2, tiled=True)  32.5 us
    all_to_all x1, blocking collectives, on_device(): lax.all_to_all(lax.all_to_all(spectra, 'inputs', split_axis=0, concat_axi...  17.4 us
    dot_general x1, matrix products, on_device(): jnp.einsum('kn,itn->kit', table, filtered, preferred_element_type=jnp.flo...  6.55 us
    unnamed x4, local copies, waits for them, and re-layouts  5.2 us
    all_to_all x2, local copies, waits for them, and re-layouts, on_device(): lax.all_to_all(spectra, 'inputs', split_axis=0, concat_axis=2, tiled=True)  3.96 us
    ppermute x1, starting transfers between devices, from_behind(): lax.ppermute(value, axis, [(source, source + steps) for source in range(i...  2.39 us
    convert_element_type x1, local copies, waits for them, and re-layouts, on_device(): spectra.astype(jnp.bfloat16).reshape(F, 2, inp_local, frames_local)  2.03 us
  transfers between devices with their start and end apart: 1, of which 0 were waited for; matrix products, arithmetic and copies ran while one was open for 1% of the time, Pallas kernels for 0%

commit v1 on v0

--- a/solution.py
+++ b/solution.py
@@ -7,6 +7,29 @@
 TAPS = 8
 TILE = 128
 FRAME = 512
+
+
+def split_up(x, dim, size):
+    shape = x.shape
+    blocks = x.reshape(*shape[:dim], size, shape[dim] // size, *shape[dim + 1 :])
+    return jnp.moveaxis(blocks, dim, 0)
+
+
+def laid_out(blocks, dim):
+    blocks = jnp.moveaxis(blocks, 0, dim)
+    dims = blocks.shape
+    return blocks.reshape(*dims[:dim], dims[dim] * dims[dim + 1], *dims[dim + 2 :])
+
+
+def exchange_directly(x, axis, split_dim, concat_dim):
+    size, index = (lax.axis_size(axis), lax.axis_index(axis))
+    blocks = split_up(x, split_dim, size)
+    done = [blocks[index]]
+    for turn in range(1, size):
+        sent = blocks[(index + turn) % size]
+        done.append(lax.ppermute(sent, axis, [(i, (i + turn) % size) for i in range(size)]))
+    blocks = jnp.stack(done)[(index - jnp.arange(size)) % size]
+    return laid_out(blocks, concat_dim)
 
 
 def from_behind(value, axis, steps):
@@ -73,11 +96,7 @@
     blocks_time = lax.axis_size("tm")
     scale = 1.0 / (frames_local * blocks_time)
     turned = lax.all_to_all(
-        lax.all_to_all(spectra, "inputs", split_axis=0, concat_axis=2, tiled=True),
-        "tm",
-        split_axis=0,
-        concat_axis=3,
-        tiled=True,
+        exchange_directly(spectra, "inputs", 0, 2), "tm", split_axis=0, concat_axis=3, tiled=True
     )
     return tile_sums(turned, scale)
 

time: 76.7 us -> 91.3 us (1.19)
  the two profiles are of different devices: /device:TPU:0 before, /device:TPU:12 now
where the time goes in v1:
time: 91.3 us; the launch traced here: 90.9 us
  waiting for transfers between devices  36.4 us (40%)
  local copies, waits for them, and re-layouts  18 us (20%)
  blocking collectives  16.9 us (19%)
  starting transfers between devices  10.5 us (12%)
  matrix products  7.41 us (8%)
  other arithmetic  1.45 us (2%)
    ppermute x7, waiting for transfers between devices, exchange_directly(): lax.ppermute(sent, axis, [(i, (i + turn) % size) for i in range(size)])  36.4 us
    all_to_all x1, blocking collectives, on_device(): lax.all_to_all(exchange_directly(spectra, 'inputs', 0, 2), 'tm', split_ax...  16.9 us
    ppermute x7, starting transfers between devices, exchange_directly(): lax.ppermute(sent, axis, [(i, (i + turn) % size) for i in range(size)])  8.74 us
    dot_general x1, matrix products, on_device(): jnp.einsum('kn,itn->kit', table, filtered, preferred_element_type=jnp.flo...  6.55 us
    unnamed x9, local copies, waits for them, and re-layouts  5.56 us
    gather x1, local copies, waits for them, and re-layouts, exchange_directly(): blocks = jnp.stack(done)[(index - jnp.arange(size)) % size]  2.54 us
    reshape x1, local copies, waits for them, and re-layouts, laid_out(): blocks.reshape(*dims[:dim], dims[dim] * dims[dim + 1], *dims[dim + 2:])  2.13 us
    convert_element_type x1, local copies, waits for them, and re-layouts, on_device(): spectra.astype(jnp.bfloat16).reshape(F, 2, inp_local, frames_local)  2.03 us
  transfers between devices with their start and end apart: 8, of which 5 were waited for; matrix products, arithmetic and copies ran while one was open for 8% of the time, Pallas kernels for 0%

profile of v1, /device:TPU:12, one launch (start us, length us, event | category | flops | bytes accessed | tf_op | source)
XLA Modules:
  0.0 90.9 jit_solution(11254391473375022890)
XLA Ops:
  0.0 0.9 slice.60
  0.9 1.7 %collective-permute-start = (bf16[16,3584]{1,0:T(8,128)(2,1)S(1)}, bf16[16,3584]{1,0:T(8,128)(2,1)S(1)}, u32[]{:S(2)}, u32[]{:S(2)}) collective-permute-start(bf16[16,3584]{1,0:T(8,128)(2,1)S(1)} %slice.60), channel_id=1, source_target_pairs={{0,1},{1,2},{2,3},{4,5},{5,6},{6,7},{8,9},{9,10},{10,11},{12,13},{... | collective-permute-start | bytes 344072 | tf_op jit(solution)/shard_map/ppermute | solution.py:38
  2.7 1.0 %fusion.34 = (f32[1,512]{1,0:T(1,128)S(1)}, f32[1,512]{1,0:T(1,128)S(1)}, f32[1,512]{1,0:T(1,128)S(1)}, f32[1,512]{1,0:T(1,128)S(1)}, f32[1,512]{1,0:T(1,128)S(1...) fusion(f32[8,512]{1,0:T(8,128)} %param.3), kind=kLoop, calls=%fused_computation.79 | loop fusion | bytes 32768 | tf_op jit(solution)/shard_map/slice | solution.py:89
  3.9 0.0 collective-permute-done
  3.9 1.3 %pad_maximum_fusion = bf16[16,36352]{1,0:T(8,128)(2,1)S(1)} fusion(bf16[16,32768]{1,0:T(8,128)(2,1)} %param.2, bf16[16,3584]{1,0:T(8,128)(2,1)S(1)} %collective-permute-done), kind=kLoop, calls=%fused_computation.8 | loop fusion | flops 2326528 | bytes 2326528 | tf_op jit(solution)/shard_map/concatenate | solution.py:84
  5.2 0.7 reshape.123
  5.9 6.5 %convolution_convert_fusion = bf16[512,16,64]{0,2,1:T(8,128)(2,1)S(1)} fusion(bf16[16,71,512]{2,1,0:T(8,128)(2,1)S(1)} %reshape.123, f32[512]{0:T(512)S(1)} %bitcast.84, f32[512]{0:T(512)S(1)} %bitcast.85, f32[512]{0:T(512)S(1)} %bitcast.79, f32[512]{0:T(512)S(1)} %bitcast.80, f32[512]{0:T(512)S(1)} %bitcast.81, f32[512]{0:T(512)S(1)} %bitcast.82, ...), kind=kOutput, calls=%fused_computation.5 | convolution fusion | flops 554696704 | bytes 9456128 | tf_op jit(solution)/shard_map/kn,itn->kit/dot_general | solution.py:94
  12.4 2.0 %copy.4 = bf16[512,16,64]{2,1,0:T(8,128)(2,1)S(1)} copy(bf16[512,16,64]{0,2,1:T(8,128)(2,1)S(1)} %convolution_convert_fusion) | data formatting | bytes 2097152 | tf_op jit(solution)/shard_map/convert_element_type | solution.py:95
  14.5 0.4 constant_dynamic-slice_fusion
  14.9 0.1 copy.35
  15.0 1.6 %collective-permute-start.1 = (bf16[32,2,16,64]{3,0,1,2:T(8,128)(2,1)S(1)}, bf16[32,2,16,64]{3,0,1,2:T(8,128)(2,1)S(1)}, u32[]{:S(2)}, u32[]{:S(2)}) collective-permute-start(bf16[32,2,16,64]{3,0,1,2:T(8,128)(2,1)S(1)} %bitcast.77), channel_id=1, source_target_pairs={{0,4},{4,8},{8,12},{12,16},{16,20},{20,24},{24,28},{28,0},{1,5},{5... | collective-permute-start | bytes 393224 | tf_op jit(solution)/shard_map/ppermute | solution.py:30
  16.5 0.1 copy.34
  16.7 1.6 %collective-permute-start.2 = (bf16[32,2,16,64]{3,0,1,2:T(8,128)(2,1)S(1)}, bf16[32,2,16,64]{3,0,1,2:T(8,128)(2,1)S(1)}, u32[]{:S(2)}, u32[]{:S(2)}) collective-permute-start(bf16[32,2,16,64]{3,0,1,2:T(8,128)(2,1)S(1)} %bitcast.76), channel_id=1, source_target_pairs={{0,8},{4,12},{8,16},{12,20},{16,24},{20,28},{24,0},{28,4},{1,9},{5... | collective-permute-start | bytes 393224 | tf_op jit(solution)/shard_map/ppermute | solution.py:30
  18.3 0.1 copy.33
  18.4 1.2 %collective-permute-start.3 = (bf16[32,2,16,64]{3,0,1,2:T(8,128)(2,1)S(1)}, bf16[32,2,16,64]{3,0,1,2:T(8,128)(2,1)S(1)}, u32[]{:S(2)}, u32[]{:S(2)}) collective-permute-start(bf16[32,2,16,64]{3,0,1,2:T(8,128)(2,1)S(1)} %bitcast.75), channel_id=1, source_target_pairs={{0,12},{4,16},{8,20},{12,24},{16,28},{20,0},{24,4},{28,8},{1,13},{... | collective-permute-start | bytes 393224 | tf_op jit(solution)/shard_map/ppermute | solution.py:30
  19.6 0.1 copy.32
  19.7 1.8 %collective-permute-start.4 = (bf16[32,2,16,64]{3,0,1,2:T(8,128)(2,1)S(1)}, bf16[32,2,16,64]{3,0,1,2:T(8,128)(2,1)S(1)}, u32[]{:S(2)}, u32[]{:S(2)}) collective-permute-start(bf16[32,2,16,64]{3,0,1,2:T(8,128)(2,1)S(1)} %bitcast.74), channel_id=1, source_target_pairs={{0,16},{4,20},{8,24},{12,28},{16,0},{20,4},{24,8},{28,12},{1,17},{... | collective-permute-start | bytes 393224 | tf_op jit(solution)/shard_map/ppermute | solution.py:30
  21.5 0.1 copy.31
  21.6 1.3 %collective-permute-start.5 = (bf16[32,2,16,64]{3,0,1,2:T(8,128)(2,1)S(1)}, bf16[32,2,16,64]{3,0,1,2:T(8,128)(2,1)S(1)}, u32[]{:S(2)}, u32[]{:S(2)}) collective-permute-start(bf16[32,2,16,64]{3,0,1,2:T(8,128)(2,1)S(1)} %bitcast.73), channel_id=1, source_target_pairs={{0,20},{4,24},{8,28},{12,0},{16,4},{20,8},{24,12},{28,16},{1,21},{... | collective-permute-start | bytes 393224 | tf_op jit(solution)/shard_map/ppermute | solution.py:30
  22.9 0.1 copy.30
  23.0 0.1 copy.29
  23.2 0.8 copy_dynamic-update-slice_fusion
  24.0 0.0 collective-permute-done.1
  24.0 1.2 %collective-permute-start.6 = (bf16[32,2,16,64]{3,0,1,2:T(8,128)(2,1)S(1)}, bf16[32,2,16,64]{3,0,1,2:T(8,128)(2,1)S(1)}, u32[]{:S(2)}, u32[]{:S(2)}) collective-permute-start(bf16[32,2,16,64]{3,0,1,2:T(8,128)(2,1)S(1)} %bitcast.72), channel_id=1, source_target_pairs={{0,24},{4,28},{8,0},{12,4},{16,8},{20,12},{24,16},{28,20},{1,25},{... | collective-permute-start | bytes 393224 | tf_op jit(solution)/shard_map/ppermute | solution.py:30
  25.2 0.7 bitcast_dynamic-update-slice_fusion.6
  25.9 2.5 %collective-permute-done.2 = bf16[32,2,16,64]{3,0,1,2:T(8,128)(2,1)S(1)} collective-permute-done((bf16[32,2,16,64]{3,0,1,2:T(8,128)(2,1)S(1)}, bf16[32,2,16,64]{3,0,1,2:T(8,128)(2,1)S(1)}, u32[]{:S(2)}, u32[]{:S(2)}) %collective-permute-start.2) | collective-permute-done | bytes 131104 | tf_op jit(solution)/shard_map/ppermute | solution.py:30
  28.4 0.0 collective-permute-start.7
  28.4 0.7 bitcast_dynamic-update-slice_fusion.5
  29.1 26.5 %collective-permute-done.3 = bf16[32,2,16,64]{3,0,1,2:T(8,128)(2,1)S(1)} collective-permute-done((bf16[32,2,16,64]{3,0,1,2:T(8,128)(2,1)S(1)}, bf16[32,2,16,64]{3,0,1,2:T(8,128)(2,1)S(1)}, u32[]{:S(2)}, u32[]{:S(2)}) %collective-permute-start.3) | collective-permute-done | bytes 131104 | tf_op jit(solution)/shard_map/ppermute | solution.py:30
  55.6 0.7 bitcast_dynamic-update-slice_fusion.4
  56.3 4.9 %collective-permute-done.4 = bf16[32,2,16,64]{3,0,1,2:T(8,128)(2,1)S(1)} collective-permute-done((bf16[32,2,16,64]{3,0,1,2:T(8,128)(2,1)S(1)}, bf16[32,2,16,64]{3,0,1,2:T(8,128)(2,1)S(1)}, u32[]{:S(2)}, u32[]{:S(2)}) %collective-permute-start.4) | collective-permute-done | bytes 131104 | tf_op jit(solution)/shard_map/ppermute | solution.py:30
  61.2 0.7 bitcast_dynamic-update-slice_fusion.3
  61.9 0.0 collective-permute-done.5
  61.9 0.7 bitcast_dynamic-update-slice_fusion.2
  62.7 1.4 %collective-permute-done.6 = bf16[32,2,16,64]{3,0,1,2:T(8,128)(2,1)S(1)} collective-permute-done((bf16[32,2,16,64]{3,0,1,2:T(8,128)(2,1)S(1)}, bf16[32,2,16,64]{3,0,1,2:T(8,128)(2,1)S(1)}, u32[]{:S(2)}, u32[]{:S(2)}) %collective-permute-start.6) | collective-permute-done | bytes 131104 | tf_op jit(solution)/shard_map/ppermute | solution.py:30
  64.1 0.7 bitcast_dynamic-update-slice_fusion.1
  64.8 1.1 %collective-permute-done.7 = bf16[32,2,16,64]{3,0,1,2:T(8,128)(2,1)S(1)} collective-permute-done((bf16[32,2,16,64]{3,0,1,2:T(8,128)(2,1)S(1)}, bf16[32,2,16,64]{3,0,1,2:T(8,128)(2,1)S(1)}, u32[]{:S(2)}, u32[]{:S(2)}) %collective-permute-start.7) | collective-permute-done | bytes 131104 | tf_op jit(solution)/shard_map/ppermute | solution.py:30
  65.9 0.7 bitcast_dynamic-update-slice_fusion
  66.7 2.5 %gather_fusion = bf16[8,32,2,16,64]{4,1,2,3,0:T(8,128)(2,1)S(1)} fusion(bf16[8,32,2,16,64]{4,1,2,3,0:T(8,128)(2,1)} %bitcast_dynamic-update-slice_fusion, s32[1024]{0:T(1024)S(1)} %pad_clamp_fusion), kind=kCustom, calls=%fused_computation | custom fusion | bytes 2097184 | tf_op jit(solution)/shard_map/gather | solution.py:31
  69.2 2.1 %copy.13 = bf16[32,2,128,64]{2,3,1,0:T(8,128)(2,1)S(1)} copy(bf16[32,2,128,64]{3,0,1,2:T(8,128)(2,1)S(1)} %bitcast.64) | data formatting | bytes 2097152 | tf_op jit(solution)/shard_map/reshape | solution.py:21
  71.4 16.9 %all_to_all.18 = bf16[32,2,128,64]{2,3,1,0:T(8,128)(2,1)S(1)} all-to-all(bf16[32,2,128,64]{2,3,1,0:T(8,128)(2,1)S(1)} %copy.13), channel_id=1, replica_groups=mesh['inputs'=8,'tm'=4] {'tm'}, dimensions={0} | all-to-all | bytes 2097152 | tf_op jit(solution)/shard_map/all_to_all | solution.py:98
  88.2 0.1 copy.14
  88.3 0.1 fusion.33
  88.4 0.2 copy.19
  88.6 0.2 copy.20
  88.9 0.4 convolution_bitcast_fusion.1
  89.3 0.4 convolution_bitcast_fusion
  89.8 0.1 maximum_multiply_fusion
  89.9 1.1 %copy.17 = f32[8,1,2,128,128]{4,3,2,1,0:T(8,128)} copy(f32[8,1,2,128,128]{4,3,0,2,1:T(8,128)S(1)} %maximum_multiply_fusion) | data formatting | bytes 2097152 | tf_op jit(solution)/shard_map/mul | solution.py:77
  (5 shorter events, 0.1 us)
Async XLA Ops:
  0.9 3.0 %collective-permute-start = (bf16[16,3584]{1,0:T(8,128)(2,1)S(1)}, bf16[16,3584]{1,0:T(8,128)(2,1)S(1)}, u32[]{:S(2)}, u32[]{:S(2)}) collective-permute-start(bf16[16,3584]{1,0:T(8,128)(2,1)S(1)} %slice.60), channel_id=1, source_target_pairs={{0,1},{1,2},{2,3},{4,5},{5,6},{6,7},{8,9},{9,10},{10,11},{12,13},{... | collective-permute-start | bytes 344072 | tf_op jit(solution)/shard_map/ppermute | solution.py:38
  15.0 9.0 %collective-permute-start.1 = (bf16[32,2,16,64]{3,0,1,2:T(8,128)(2,1)S(1)}, bf16[32,2,16,64]{3,0,1,2:T(8,128)(2,1)S(1)}, u32[]{:S(2)}, u32[]{:S(2)}) collective-permute-start(bf16[32,2,16,64]{3,0,1,2:T(8,128)(2,1)S(1)} %bitcast.77), channel_id=1, source_target_pairs={{0,4},{4,8},{8,12},{12,16},{16,20},{20,24},{24,28},{28,0},{1,5},{5... | collective-permute-start | bytes 393224 | tf_op jit(solution)/shard_map/ppermute | solution.py:30
  16.7 11.8 %collective-permute-start.2 = (bf16[32,2,16,64]{3,0,1,2:T(8,128)(2,1)S(1)}, bf16[32,2,16,64]{3,0,1,2:T(8,128)(2,1)S(1)}, u32[]{:S(2)}, u32[]{:S(2)}) collective-permute-start(bf16[32,2,16,64]{3,0,1,2:T(8,128)(2,1)S(1)} %bitcast.76), channel_id=1, source_target_pairs={{0,8},{4,12},{8,16},{12,20},{16,24},{20,28},{24,0},{28,4},{1,9},{5... | collective-permute-start | bytes 393224 | tf_op jit(solution)/shard_map/ppermute | solution.py:30
  18.4 37.2 %collective-permute-start.3 = (bf16[32,2,16,64]{3,0,1,2:T(8,128)(2,1)S(1)}, bf16[32,2,16,64]{3,0,1,2:T(8,128)(2,1)S(1)}, u32[]{:S(2)}, u32[]{:S(2)}) collective-permute-start(bf16[32,2,16,64]{3,0,1,2:T(8,128)(2,1)S(1)} %bitcast.75), channel_id=1, source_target_pairs={{0,12},{4,16},{8,20},{12,24},{16,28},{20,0},{24,4},{28,8},{1,13},{... | collective-permute-start | bytes 393224 | tf_op jit(solution)/shard_map/ppermute | solution.py:30
  19.7 41.5 %collective-permute-start.4 = (bf16[32,2,16,64]{3,0,1,2:T(8,128)(2,1)S(1)}, bf16[32,2,16,64]{3,0,1,2:T(8,128)(2,1)S(1)}, u32[]{:S(2)}, u32[]{:S(2)}) collective-permute-start(bf16[32,2,16,64]{3,0,1,2:T(8,128)(2,1)S(1)} %bitcast.74), channel_id=1, source_target_pairs={{0,16},{4,20},{8,24},{12,28},{16,0},{20,4},{24,8},{28,12},{1,17},{... | collective-permute-start | bytes 393224 | tf_op jit(solution)/shard_map/ppermute | solution.py:30
  21.6 40.4 %collective-permute-start.5 = (bf16[32,2,16,64]{3,0,1,2:T(8,128)(2,1)S(1)}, bf16[32,2,16,64]{3,0,1,2:T(8,128)(2,1)S(1)}, u32[]{:S(2)}, u32[]{:S(2)}) collective-permute-start(bf16[32,2,16,64]{3,0,1,2:T(8,128)(2,1)S(1)} %bitcast.73), channel_id=1, source_target_pairs={{0,20},{4,24},{8,28},{12,0},{16,4},{20,8},{24,12},{28,16},{1,21},{... | collective-permute-start | bytes 393224 | tf_op jit(solution)/shard_map/ppermute | solution.py:30
  24.0 40.1 %collective-permute-start.6 = (bf16[32,2,16,64]{3,0,1,2:T(8,128)(2,1)S(1)}, bf16[32,2,16,64]{3,0,1,2:T(8,128)(2,1)S(1)}, u32[]{:S(2)}, u32[]{:S(2)}) collective-permute-start(bf16[32,2,16,64]{3,0,1,2:T(8,128)(2,1)S(1)} %bitcast.72), channel_id=1, source_target_pairs={{0,24},{4,28},{8,0},{12,4},{16,8},{20,12},{24,16},{28,20},{1,25},{... | collective-permute-start | bytes 393224 | tf_op jit(solution)/shard_map/ppermute | solution.py:30
  28.4 37.5 %collective-permute-start.7 = (bf16[32,2,16,64]{3,0,1,2:T(8,128)(2,1)S(1)}, bf16[32,2,16,64]{3,0,1,2:T(8,128)(2,1)S(1)}, u32[]{:S(2)}, u32[]{:S(2)}) collective-permute-start(bf16[32,2,16,64]{3,0,1,2:T(8,128)(2,1)S(1)} %bitcast.71), channel_id=1, source_target_pairs={{0,28},{4,0},{8,4},{12,8},{16,12},{20,16},{24,20},{28,24},{1,29},{... | collective-permute-start | bytes 393224 | tf_op jit(solution)/shard_map/ppermute | solution.py:30
